TPU v7x, 256 devices: a whole 4x4x8 slice. The times are simulated.
256 devices in a mesh: dp: 8 (over x_hi, y), fsdp: 16 (over z, core), tensor: 2 (over x_lo).
Axes of the slice: x: 4 (x_hi: 2, x_lo: 2; x = x_hi * 2 + x_lo), y: 4, z: 8, core: 2. Of those that a mesh axis runs over, the one named last changes fastest.
Arguments:
- attn_out: bfloat16 [16384, 2560], P(('dp', 'fsdp')), may hold values from -6 to 6
- cotangent: bfloat16 [16384, 5120], P(('dp', 'fsdp'), 'tensor'), may hold values from -6 to 6
- old_weights: bfloat16 [3, 2048, 4096], P(None, 'tensor', 'fsdp'), may hold values from -0.125 to 0.125
- depth_coef: float32 [2], replicated, may hold values from 0.3 to 1
- depth_pick: int32 [2], replicated, may hold values from 0 to 2
- in_blocks: bfloat16 [20, 2, 128, 128], replicated, may hold values from -0.3125 to 0.3125
- in_cols: int32 [20, 2], replicated, may hold values from 0 to 15, all different within a row
- out_blocks: bfloat16 [40, 2, 128, 128], P('tensor'), may hold values from -0.375 to 0.375
- out_cols: int32 [40, 2], P('tensor'), may hold values from 0 to 31, all different within a row
Outputs:
- grown_out: bfloat16 [16384, 5120], P(('dp', 'fsdp'), 'tensor')
- grad_attn: bfloat16 [16384, 2560], P(('dp', 'fsdp'), 'tensor')
- grad_in_blocks: float32 [20, 2, 128, 128], P('tensor')
- grad_out_blocks: float32 [40, 2, 128, 128], P('tensor')
Inputs may be any that keep to these rules, and one draw needn't show every extreme that they name: `in_cols`: each row names 2 different old head blocks; every old head block is named by some row. `out_cols`: each row names 2 different old width blocks; every old width block is named by some row.
All inputs are finite; a program needn't handle non-finite values.
Results may differ from a plain program's by a relative error of at most 0.0095.
Values may be sent and summed in bfloat16 or wider, within the bound.
No kernel may reach another device: no remote copies, remote signals or barrier semaphores. Data moves between devices by JAX's collectives and lax.ppermute only.
A program may use at most 64 MiB of HBM per device.

v0:
```python
import jax
import jax.numpy as jnp
from jax import lax
from jax.sharding import PartitionSpec as P

HEAD = 128
D_OLD = 4096
HG_OLD = 16
HG_NEW = 20
DEPTH_K = 2
BO_OLD = 32


def gathered_mix(mixed_weight):
    return lax.all_gather(mixed_weight, "fsdp", axis=1, tiled=True)


def local(
    attn_out,
    cotangent,
    old_weights,
    depth_coef,
    depth_pick,
    in_blocks,
    in_cols,
    out_blocks,
    out_cols,
):
    highest = lax.Precision.HIGHEST
    tok_rows = attn_out.shape[0]
    tensor_half = lax.axis_index("tensor")
    tensor_count = lax.axis_size("tensor")
    local_old = old_weights.shape[1]
    local_blocks = local_old // HEAD
    rows_in = HG_NEW // tensor_count
    mixed_weight = jnp.zeros(old_weights.shape[1:], jnp.float32)
    for layer_slot in range(DEPTH_K):
        picked = lax.dynamic_index_in_dim(old_weights, depth_pick[layer_slot], 0, keepdims=False)
        mixed_weight = mixed_weight + depth_coef[layer_slot] * picked.astype(jnp.float32)
    mixed_weight = mixed_weight.astype(jnp.bfloat16)
    attn_blocks = attn_out.reshape(tok_rows, HG_NEW, HEAD)
    products = jnp.einsum(
        "trd,rkde->trke", attn_blocks, in_blocks, preferred_element_type=jnp.float32
    )
    local_cols = tensor_half * local_blocks + jnp.arange(local_blocks, dtype=jnp.int32)
    in_hot = (in_cols[:, :, None] == local_cols[None, None, :]).astype(jnp.float32)
    hidden_local = jnp.einsum("trke,rkc->tce", products, in_hot, precision=highest)
    hidden_local = hidden_local.reshape(tok_rows, local_old).astype(jnp.bfloat16)
    full_mix = gathered_mix(mixed_weight)
    old_part = jnp.dot(hidden_local, full_mix, preferred_element_type=jnp.float32)
    old_out = lax.psum(old_part.astype(jnp.bfloat16), "tensor")
    old_selected = jnp.take(old_out.reshape(tok_rows, BO_OLD, HEAD), out_cols, axis=1)
    grown_out = jnp.einsum(
        "trkd,rkde->tre", old_selected, out_blocks, preferred_element_type=jnp.float32
    )
    grown_out = grown_out.reshape(tok_rows, -1).astype(jnp.bfloat16)
    cot_blocks = cotangent.reshape(tok_rows, out_blocks.shape[0], HEAD)
    backward_terms = jnp.einsum(
        "tre,rkde->trkd", cot_blocks, out_blocks, preferred_element_type=jnp.float32
    )
    out_hot = (out_cols[:, :, None] == jnp.arange(BO_OLD, dtype=jnp.int32)[None, None, :]).astype(
        jnp.float32
    )
    grad_part = jnp.einsum("trkd,rkc->tcd", backward_terms, out_hot, precision=highest).reshape(
        tok_rows, D_OLD
    )
    old_grad = lax.psum(grad_part.astype(jnp.bfloat16), "tensor")
    hidden_grad_local = jnp.einsum(
        "to,fo->tf", old_grad, full_mix, preferred_element_type=jnp.float32
    ).astype(jnp.bfloat16)
    hidden_grad = lax.all_gather(hidden_grad_local, "tensor", axis=1, tiled=True)
    my_in_blocks = lax.dynamic_slice_in_dim(in_blocks, tensor_half * rows_in, rows_in, 0)
    my_in_cols = lax.dynamic_slice_in_dim(in_cols, tensor_half * rows_in, rows_in, 0)
    grad_selected = jnp.take(hidden_grad.reshape(tok_rows, HG_OLD, HEAD), my_in_cols, axis=1)
    grad_attn = jnp.einsum(
        "trke,rkde->trd", grad_selected, my_in_blocks, preferred_element_type=jnp.float32
    )
    grad_attn = grad_attn.reshape(tok_rows, rows_in * HEAD).astype(jnp.bfloat16)
    my_attn = lax.dynamic_slice_in_dim(attn_blocks, tensor_half * rows_in, rows_in, 1)
    in_terms = jnp.einsum(
        "trd,trke->rkde", my_attn, grad_selected, preferred_element_type=jnp.float32
    )
    out_terms = jnp.einsum(
        "trkd,tre->rkde", old_selected, cot_blocks, preferred_element_type=jnp.float32
    )
    in_sum, out_sum = lax.psum((in_terms, out_terms), ("dp", "fsdp"))
    grad_scale = float(tok_rows * lax.axis_size("dp") * lax.axis_size("fsdp")) ** (-0.5)
    return (grown_out, grad_attn, in_sum * grad_scale, out_sum * grad_scale)


def solution(mesh):
    placed = (
        P(("dp", "fsdp"), None),
        P(("dp", "fsdp"), "tensor"),
        P(None, "tensor", "fsdp"),
        P(),
        P(),
        P(),
        P(),
        P("tensor", None, None, None),
        P("tensor", None),
    )
    return jax.shard_map(
        local,
        mesh=mesh,
        in_specs=placed,
        out_specs=(
            P(("dp", "fsdp"), "tensor"),
            P(("dp", "fsdp"), "tensor"),
            P("tensor", None, None, None),
            P("tensor", None, None, None),
        ),
        check_vma=False,
    )
```

profile of v0, /device:TPU:6, one launch (start us, length us, event | category | flops | bytes accessed | tf_op | source)
XLA Modules:
  0.0 1481.5 jit_solution(9573268355496351866)
XLA Ops:
  7.2 0.0 copy-start
  7.2 0.0 all-gather.3.cloned.1.call-start
  7.2 1.3 fusion.55
  11.2 1.3 fusion.54
  13.8 3.5 add_convert_fusion
  17.3 0.0 all-gather.3.cloned.1.call-update
  17.4 0.0 all-reduce.7.cloned.1.call-start
  17.4 1.5 copy.27
  18.9 2.0 fusion.56
  21.0 3.6 copy.45
  24.6 0.3 copy.34
  24.9 2.0 fusion.57
  26.9 3.6 copy.51
  30.5 3.5 bitcast_convert_fusion
  34.0 1.4 copy.71
  35.5 3.0 fusion.24
  38.5 46.0 %all-gather.3.cloned.1.call-done = bf16[1,1024,4096]{2,1,0:T(8,128)(2,1)} async-done(((bf16[1,1024,256]{2,1,0:T(8,128)(2,1)}), bf16[1,1024,4096]{2,1,0:T(8,128)(2,1)}) %all-gather.3.cloned.1.call-update) | async-done | bytes 8388624 | tf_op jit(solution)/shard_map/all_gather | solution.py:15
  84.5 4.7 fusion.13
  89.1 1.3 copy.72
  90.4 0.0 all-reduce.7.cloned.1.call-update
  90.4 0.0 all-reduce.5.cloned.1.call-start
  90.5 0.1 compare_and_fusion
  90.6 0.1 copy.35
  90.7 0.1 reshape.66
  90.7 0.1 copy.33
  90.8 0.1 copy.29
  91.0 0.1 reshape.58
  91.1 0.1 copy.26
  91.2 72.4 %all-reduce.7.cloned.1.call-done = (bf16[128,32,128]{2,0,1:T(8,128)(2,1)}, bf16[128,4096]{1,0:T(8,128)(2,1)}) async-done(((bf16[128,32,128]{2,0,1:T(8,128)(2,1)}, bf16[128,4096]{1,0:T(8,128)(2,1)}), (bf16[128,32,128]{2,0,1:T(8,128)(2,1)}, bf16[128,4096]{1,0:T(8,128)(2,1)})) %all-reduce.7.cloned.1.call-update) | async-done | bytes 2097168 | tf_op jit(solution)/shard_map/psum | solution.py:51
  163.5 6.6 fusion.27
  170.2 8.7 all_gather.7
  178.9 0.1 copy_bitcast_fusion.2
  179.0 0.7 gather_fusion.1
  179.7 1.1 copy.37
  180.8 3.1 gather_fusion
  183.9 1.8 copy.30
  185.7 2.0 fusion.17
  187.7 1.4 convolution_bitcast_fusion
  189.1 0.0 all-reduce.5.cloned.1.call-update
  189.2 1.1 copy-done.4
  190.2 2.2 fusion.23
  192.4 1.9 copy.42
  194.3 0.6 fusion.16
  194.9 1.1 copy.41
  196.0 1273.8 %all-reduce.5.cloned.1.call-done = (f32[10,2,128,128]{2,3,1,0:T(8,128)}, f32[20,2,128,128]{3,2,1,0:T(8,128)}) async-done(((f32[10,2,128,128]{2,3,1,0:T(8,128)}, f32[20,2,128,128]{3,2,1,0:T(8,128)}), (f32[10,2,128,128]{2,3,1,0:T(8,128)}, f32[20,2,128,128]{3,2,1,0:T(8,128)})) %all-reduce.5.cloned.1.call-update) | async-done | bytes 3932176 | tf_op jit(solution)/shard_map/psum | solution.py:86
  1469.8 3.6 broadcast_multiply_fusion
  1473.4 0.1 broadcast_multiply_fusion.1
  1473.5 1.5 copy.43
  (23 shorter events, 0.1 us)
Async XLA Ops:
  7.2 17.8 %copy-start = (bf16[20,2,128,128]{3,2,1,0:T(8,128)(2,1)S(1)}, bf16[20,2,128,128]{3,2,1,0:T(8,128)(2,1)}, u32[]{:S(2)}) copy-start(bf16[20,2,128,128]{3,2,1,0:T(8,128)(2,1)} %param.16) | copy-start | bytes 3932164
  7.2 77.3 %all-gather.3.cloned.1.call-start = ((), (), s32[]{:S(2)}) async-start(), calls=%async_computation | async-start | bytes 8912896 | tf_op jit(solution)/shard_map/all_gather | solution.py:15
  17.3 1.6 copy-start.6
  17.4 146.2 %all-reduce.7.cloned.1.call-start = ((), (), s32[]{:S(2)}) async-start(), calls=%async_computation.2 | async-start | bytes 4194304 | tf_op jit(solution)/shard_map/psum | solution.py:51
  18.9 2.1 copy-start.1
  21.0 3.6 copy-start.7
  26.9 3.6 copy-start.9
  34.0 1.4 copy-start.8
  90.4 1379.4 %all-reduce.5.cloned.1.call-start = ((), (), s32[]{:S(2)}) async-start(), calls=%async_computation.1 | async-start | bytes 7864320 | tf_op jit(solution)/shard_map/psum | solution.py:86
  185.6 2.1 copy-start.2
  185.6 2.1 copy-start.3
  189.1 1.1 copy-start.4
  1469.8 3.6 copy-start.5
Sparse Core Ops, SparseCore 0:
  17.5 66.9 all-gather.2
  90.5 72.9 all-reduce.6
  189.3 1280.4 all-reduce.4
where the time goes:
time: 1480 us
  waiting for transfers between devices  1390 us (94%)
  matrix products  28.2 us (2%)
  local copies, waits for them, and re-layouts  27.2 us (2%)
  between operations  17.8 us (1%)
    psum x1, waiting for transfers between devices, local(): in_sum, out_sum = lax.psum((in_terms, out_terms), ('dp', 'fsdp'))  1270 us
    psum x1, waiting for transfers between devices, local(): old_out = lax.psum(old_part.astype(jnp.bfloat16), 'tensor')  72.4 us
    all_gather x1, waiting for transfers between devices, gathered_mix(): return lax.all_gather(mixed_weight, 'fsdp', axis=1, tiled=True)  46 us
  transfers between devices with their start and end apart: 3, of which 3 were waited for; matrix products, arithmetic and copies ran while one was open for 2% of the time, Pallas kernels for 0%

commit v1 on v0

--- a/solution.py
+++ b/solution.py
@@ -9,6 +9,7 @@
 HG_NEW = 20
 DEPTH_K = 2
 BO_OLD = 32
+units_register = lambda xs: jax.lax.psum(jax.lax.psum(xs, "fsdp"), "dp")
 
 
 def gathered_mix(mixed_weight):
@@ -83,7 +84,7 @@
     out_terms = jnp.einsum(
         "trkd,tre->rkde", old_selected, cot_blocks, preferred_element_type=jnp.float32
     )
-    in_sum, out_sum = lax.psum((in_terms, out_terms), ("dp", "fsdp"))
+    in_sum, out_sum = units_register((in_terms, out_terms))
     grad_scale = float(tok_rows * lax.axis_size("dp") * lax.axis_size("fsdp")) ** (-0.5)
     return (grown_out, grad_attn, in_sum * grad_scale, out_sum * grad_scale)
 

time: 1480 us -> 439 us (0.30)
  waiting for transfers between devices: 1390 us -> 347 us
    psum x1 -> x2, waiting for transfers between devices: 1270 us -> 229 us  [units_register = lambda xs: jax.lax.psum(jax.lax.psum(xs, 'fsdp'), 'dp')]
  transfers between devices with their start and end apart: 3 -> 4, of which waited for: 3 -> 4; matrix products, arithmetic and copies ran while one was open for 2% -> 6% of each run, Pallas kernels for 0% -> 0%
where the time goes in v1:
time: 439 us; the launch traced here: 437 us
  waiting for transfers between devices  347 us (79%)
  matrix products  28.2 us (6%)
  local copies, waits for them, and re-layouts  27.1 us (6%)
  between operations  17.8 us (4%)
  blocking collectives  8.54 us (2%)
  other arithmetic  7.38 us (2%)
    psum x2, waiting for transfers between devices, units_register = lambda xs: jax.lax.psum(jax.lax.psum(xs, 'fsdp'), 'dp')  229 us
    psum x1, waiting for transfers between devices, local(): old_out = lax.psum(old_part.astype(jnp.bfloat16), 'tensor')  72.7 us
    all_gather x1, waiting for transfers between devices, gathered_mix(): return lax.all_gather(mixed_weight, 'fsdp', axis=1, tiled=True)  46 us
  transfers between devices with their start and end apart: 4, of which 4 were waited for; matrix products, arithmetic and copies ran while one was open for 6% of the time, Pallas kernels for 0%

profile of v1, /device:TPU:6, one launch (start us, length us, event | category | flops | bytes accessed | tf_op | source)
XLA Modules:
  0.0 436.5 jit_solution(8258386780648789214)
XLA Ops:
  7.2 0.0 all-gather.3.cloned.1.call-start
  7.2 1.3 fusion.55
  11.2 1.3 fusion.54
  13.8 3.5 add_convert_fusion
  17.3 0.0 all-gather.3.cloned.1.call-update
  17.4 0.0 all-reduce.11.cloned.1.call-start
  17.4 1.5 copy.27
  18.9 2.0 fusion.56
  21.0 3.6 copy.45
  24.6 0.3 copy.34
  24.9 2.0 fusion.57
  26.9 3.6 copy.51
  30.4 3.5 bitcast_convert_fusion
  34.0 1.4 copy.71
  35.4 3.0 fusion.24
  38.4 46.0 %all-gather.3.cloned.1.call-done = bf16[1,1024,4096]{2,1,0:T(8,128)(2,1)} async-done(((bf16[1,1024,256]{2,1,0:T(8,128)(2,1)}), bf16[1,1024,4096]{2,1,0:T(8,128)(2,1)}) %all-gather.3.cloned.1.call-update) | async-done | bytes 8388624 | tf_op jit(solution)/shard_map/all_gather | solution.py:16
  84.4 4.7 %fusion.13 = bf16[16,32,8,128]{3,2,1,0:T(8,128)(2,1)S(1)} fusion(bf16[1,1024,4096]{2,1,0:T(8,128)(2,1)} %all-gather.3.cloned.1.call-done, bf16[16,8,8,128]{3,2,1,0:T(8,128)(2,1)S(1)} %bitcast.126), kind=kOutput, calls=%fused_computation.14 | convolution fusion | flops 1074266112 | bytes 9699328 | tf_op jit(solution)/shard_map/dot_general | solution.py:51
  89.1 1.3 copy.72
  90.4 0.0 all-reduce.11.cloned.1.call-update
  90.4 0.0 all-reduce.7.cloned.1.call-start
  90.4 0.1 compare_and_fusion
  90.5 0.1 copy.35
  90.6 0.1 reshape.66
  90.7 0.1 copy.33
  90.8 0.1 copy.29
  90.9 0.1 reshape.58
  91.0 0.1 copy.26
  91.2 72.7 %all-reduce.11.cloned.1.call-done = (bf16[128,32,128]{2,0,1:T(8,128)(2,1)}, bf16[128,4096]{1,0:T(8,128)(2,1)}) async-done(((bf16[128,32,128]{2,0,1:T(8,128)(2,1)}, bf16[128,4096]{1,0:T(8,128)(2,1)}), (bf16[128,32,128]{2,0,1:T(8,128)(2,1)}, bf16[128,4096]{1,0:T(8,128)(2,1)})) %all-reduce.11.cloned.1.call-update) | async-done | bytes 2097168 | tf_op jit(solution)/shard_map/psum | solution.py:52
  163.9 6.6 %fusion.27 = bf16[128,1024]{1,0:T(8,128)(2,1)S(1)} fusion(bf16[128,4096]{1,0:T(8,128)(2,1)} %get-tuple-element.17, bf16[1,1024,4096]{2,1,0:T(8,128)(2,1)} %all-gather.3.cloned.1.call-done), kind=kOutput, calls=%fused_computation.25 | convolution fusion | flops 1073872896 | bytes 9699328 | tf_op jit(solution)/shard_map/to,fo->tf/dot_general | solution.py:69
  170.5 8.5 %all_gather.7 = bf16[128,2048]{1,0:T(8,128)(2,1)S(1)} all-gather(bf16[128,1024]{1,0:T(8,128)(2,1)S(1)} %fusion.27), channel_id=1, replica_groups=mesh['dp'=8,'fsdp'=16,'tensor'=2] {'tensor'}, dimensions={1}, use_global_device_ids=true | all-gather | bytes 786432 | tf_op jit(solution)/shard_map/all_gather | solution.py:72
  179.1 0.1 copy_bitcast_fusion.2
  179.2 0.7 gather_fusion.1
  179.9 1.1 copy.37
  181.0 3.1 gather_fusion
  184.0 1.8 copy.30
  185.8 2.0 fusion.17
  187.9 1.4 convolution_bitcast_fusion
  189.3 0.0 all-reduce.9.cloned.1.call-start
  189.4 122.8 %all-reduce.7.cloned.1.call-done = (f32[10,2,128,128]{2,3,1,0:T(8,128)}, f32[20,2,128,128]{3,2,1,0:T(8,128)}) async-done(((f32[10,2,128,128]{2,3,1,0:T(8,128)}, f32[20,2,128,128]{3,2,1,0:T(8,128)}), (f32[10,2,128,128]{2,3,1,0:T(8,128)}, f32[20,2,128,128]{3,2,1,0:T(8,128)})) %all-reduce.7.cloned.1.call-update) | async-done | bytes 3932176 | tf_op jit(solution)/shard_map/psum | solution.py:12
  312.2 1.1 copy-done.4
  313.3 2.2 fusion.23
  315.5 1.9 copy.42
  317.3 0.6 fusion.16
  318.0 1.1 copy.41
  319.1 105.7 %all-reduce.9.cloned.1.call-done = (f32[10,2,128,128]{2,3,1,0:T(8,128)}, f32[20,2,128,128]{3,2,1,0:T(8,128)}) async-done(((f32[10,2,128,128]{2,3,1,0:T(8,128)}, f32[20,2,128,128]{3,2,1,0:T(8,128)}), (f32[10,2,128,128]{2,3,1,0:T(8,128)}, f32[20,2,128,128]{3,2,1,0:T(8,128)})) %all-reduce.9.cloned.1.call-update) | async-done | bytes 3932176 | tf_op jit(solution)/shard_map/psum | solution.py:12
  424.8 3.6 broadcast_multiply_fusion
  428.4 0.1 broadcast_multiply_fusion.1
  428.5 1.5 copy.43
  (26 shorter events, 0.1 us)
Async XLA Ops:
  7.2 17.7 %copy-start = (bf16[20,2,128,128]{3,2,1,0:T(8,128)(2,1)S(1)}, bf16[20,2,128,128]{3,2,1,0:T(8,128)(2,1)}, u32[]{:S(2)}) copy-start(bf16[20,2,128,128]{3,2,1,0:T(8,128)(2,1)} %param.16) | copy-start | bytes 3932164
  7.2 77.2 %all-gather.3.cloned.1.call-start = ((), (), s32[]{:S(2)}) async-start(), calls=%async_computation | async-start | bytes 8912896 | tf_op jit(solution)/shard_map/all_gather | solution.py:16
  17.3 1.6 copy-start.6
  17.4 146.5 %all-reduce.11.cloned.1.call-start = ((), (), s32[]{:S(2)}) async-start(), calls=%async_computation.3 | async-start | bytes 4194304 | tf_op jit(solution)/shard_map/psum | solution.py:52
  18.9 2.1 copy-start.1
  21.0 3.6 copy-start.7
  26.9 3.6 copy-start.9
  34.0 1.4 copy-start.8
  90.4 221.8 %all-reduce.7.cloned.1.call-start = ((), (), s32[]{:S(2)}) async-start(), calls=%async_computation.1 | async-start | bytes 7864320 | tf_op jit(solution)/shard_map/psum | solution.py:12
  185.8 2.1 copy-start.2
  185.8 2.1 copy-start.3
  189.3 235.5 %all-reduce.9.cloned.1.call-start = ((), (), s32[]{:S(2)}) async-start(), calls=%async_computation.2 | async-start | bytes 7864320 | tf_op jit(solution)/shard_map/psum | solution.py:12
  312.2 1.1 copy-start.4
  424.8 3.6 copy-start.5
Sparse Core Ops, SparseCore 0:
  17.5 66.9 all-gather.2
  90.5 73.3 all-reduce.10
  189.5 122.6 all-reduce.6
  314.8 109.9 all-reduce.8
